TPU v7x, 32 devices: a whole 2x2x4 slice. The times are simulated.
32 devices in a mesh: groups: 2 (over y), seq: 4 (over z), proj: 2 (over x), chan: 2 (over core).
Axes of the slice: x: 2, y: 2, z: 4, core: 2. Of those that a mesh axis runs over, the one named last changes fastest.
Arguments:
- tokens: bfloat16 [8192, 8192], P('seq', ('proj', 'chan')), may hold values from -6 to 6
- w_proj: bfloat16 [8192, 3, 512], P('proj', None, ('groups', 'chan')), parts along dimension 2, may hold values from -0.0625 to 0.0625
- short_taps: float32 [3, 3, 512], P(None, None, ('groups', 'chan')), parts along dimension 2, may hold values from -3 to 3
- long_filter: bfloat16 [8192, 512], P(('seq', 'proj'), ('groups', 'chan')), parts along dimension 1, may hold values from -0.0625 to 0.0625
- filter_bias: float32 [512], P(('groups', 'chan')), parts along dimension 0, may hold values from -1 to 1
Outputs:
- mixed: bfloat16 [8192, 512], P(('seq', 'proj'), ('groups', 'chan')), parts along dimension 1
There are 2 independent parts, one for each index of `groups`. A program takes and returns all parts, laid end to end along the dimension named above; an argument that names none is the same for every part. Nothing has to cross between parts.
All inputs are finite; a program needn't handle non-finite values.
Results may differ from a plain program's by a relative error of at most 0.0075.
Values may be sent and summed in bfloat16 or wider, within the bound.
No kernel may reach another device: no remote copies, remote signals or barrier semaphores. Data moves between devices by JAX's collectives and lax.ppermute only.
A program may use at most 128 MiB of HBM per device.

v0:
```python
import math
import jax
import jax.numpy as jnp
from jax import lax
from jax.sharding import PartitionSpec as P

precise = lax.Precision.HIGH


def shifted(array, axis, by):
    size = lax.axis_size(axis)
    pairs = [(i, i + by) for i in range(size) if 0 <= i + by < size]
    return lax.ppermute(array, axis, pairs)


def twist_angles(outer, inner, total):
    outer_ids = lax.broadcasted_iota(jnp.int32, (outer, inner), 0)
    inner_ids = lax.broadcasted_iota(jnp.int32, (outer, inner), 1)
    return (outer_ids * inner_ids % total).astype(jnp.float32) * (2.0 * math.pi / total)


def dft_tables(points, direction):
    phases = twist_angles(points, points, points)
    return (jnp.cos(phases), direction * jnp.sin(phases))


def complex_einsum(form, left_re, left_im, right_re, right_im):
    real_out = jnp.einsum(form, left_re, right_re, precision=precise) - jnp.einsum(
        form, left_im, right_im, precision=precise
    )
    imag_out = jnp.einsum(form, left_re, right_im, precision=precise) + jnp.einsum(
        form, left_im, right_re, precision=precise
    )
    return (real_out, imag_out)


def rotate(data_re, data_im, turn_angle):
    cosine = jnp.cos(turn_angle)
    sine_part = jnp.sin(turn_angle)
    return (data_re * cosine - data_im * sine_part, data_re * sine_part + data_im * cosine)


def spectral_product(data_re, data_im, width, along):
    first_re = lax.slice_in_dim(data_re, 0, 2 * width, axis=along)
    first_im = lax.slice_in_dim(data_im, 0, 2 * width, axis=along)
    second_re = lax.slice_in_dim(data_re, 2 * width, 4 * width, axis=along)
    second_im = lax.slice_in_dim(data_im, 2 * width, 4 * width, axis=along)
    return (
        first_re * second_re - first_im * second_im,
        first_re * second_im + first_im * second_re,
    )


def combine_halves(time_re, time_im, width, turn_angle, along):
    even_part = lax.slice_in_dim(time_re, 0, width, axis=along)
    odd_re = lax.slice_in_dim(time_re, width, 2 * width, axis=along)
    odd_im = lax.slice_in_dim(time_im, width, 2 * width, axis=along)
    return 0.5 * (even_part + jnp.cos(turn_angle) * odd_re - jnp.sin(turn_angle) * odd_im)


def shards(tokens, w_proj, short_taps, long_filter, filter_bias):
    whole_cols = lax.all_gather(tokens, "chan", axis=1, tiled=True)
    width_in, triple, channels = w_proj.shape
    weights = w_proj.reshape(width_in, triple * channels)
    parts_proj = lax.axis_size("proj")
    rows_own = tokens.shape[0] // parts_proj
    projected = lax.psum_scatter(
        jnp.dot(whole_cols, weights, preferred_element_type=jnp.float32),
        "proj",
        scatter_dimension=0,
        tiled=True,
    )
    tap_count = short_taps.shape[0]
    taps_flat = short_taps.reshape(tap_count, triple * channels)
    tail_rows = projected[rows_own - (tap_count - 1) :]
    earlier = shifted(tail_rows, ("seq", "proj"), 1)
    extended = jnp.concatenate([earlier, projected], axis=0)
    featured = taps_flat[0] * projected
    for lag_step in range(1, tap_count):
        featured = (
            featured
            + taps_flat[lag_step]
            * extended[tap_count - 1 - lag_step : tap_count - 1 - lag_step + rows_own]
        )
    query_part = featured[:, :channels]
    gated_low = (featured[:, channels : 2 * channels] * featured[:, 2 * channels :]).astype(
        jnp.bfloat16
    )
    gated_rows = gated_low.astype(jnp.float32)
    devices = lax.axis_size(("seq", "proj"))
    seq_len = devices * rows_own
    per_device = channels // devices
    gated_low_cols, filter_low_cols = (
        lax.all_to_all(gated_low.T, ("seq", "proj"), split_axis=0, concat_axis=1, tiled=True),
        lax.all_to_all(long_filter.T, ("seq", "proj"), split_axis=0, concat_axis=1, tiled=True),
    )
    gated_cols = gated_low_cols.astype(jnp.float32)
    filter_cols = filter_low_cols.astype(jnp.float32)
    full_angle = lax.broadcasted_iota(jnp.int32, (1, seq_len), 1).astype(jnp.float32) * (
        math.pi / seq_len
    )
    zero_cols = jnp.zeros_like(gated_cols)
    umod_re, umod_im = rotate(gated_cols, zero_cols, -full_angle)
    hmod_re, hmod_im = rotate(filter_cols, zero_cols, -full_angle)
    series_re = jnp.concatenate([gated_cols, umod_re, filter_cols, hmod_re], axis=0)
    series_im = jnp.concatenate([zero_cols, umod_im, zero_cols, hmod_im], axis=0)
    grid_re = series_re.reshape(4 * per_device, devices, rows_own)
    grid_im = series_im.reshape(4 * per_device, devices, rows_own)
    outer_re, outer_im = dft_tables(devices, -1.0)
    inner_re, inner_im = dft_tables(rows_own, -1.0)
    twist = twist_angles(devices, rows_own, seq_len)
    grid_re, grid_im = complex_einsum("kd,cdj->ckj", outer_re, outer_im, grid_re, grid_im)
    grid_re, grid_im = rotate(grid_re, grid_im, -twist)
    grid_re, grid_im = complex_einsum("ckj,jq->ckq", grid_re, grid_im, inner_re, inner_im)
    spec_re, spec_im = spectral_product(grid_re, grid_im, per_device, 0)
    back_inner_re, back_inner_im = dft_tables(rows_own, 1.0)
    back_outer_re, back_outer_im = dft_tables(devices, 1.0)
    back_re, back_im = complex_einsum("ckq,qj->ckj", spec_re, spec_im, back_inner_re, back_inner_im)
    back_re, back_im = rotate(back_re, back_im, twist)
    back_re, back_im = complex_einsum("dk,ckj->cdj", back_outer_re, back_outer_im, back_re, back_im)
    time_re = back_re.reshape(2 * per_device, seq_len) * (1.0 / seq_len)
    time_im = back_im.reshape(2 * per_device, seq_len) * (1.0 / seq_len)
    long_cols = combine_halves(time_re, time_im, per_device, full_angle, 0)
    long_rows = lax.all_to_all(long_cols, ("seq", "proj"), split_axis=1, concat_axis=0, tiled=True)
    long_conv = long_rows.T
    result = query_part * (long_conv + filter_bias * gated_rows)
    return result.astype(jnp.bfloat16)


def solution(mesh):
    placed = (
        P("seq", ("proj", "chan")),
        P("proj", None, ("groups", "chan")),
        P(None, None, ("groups", "chan")),
        P(("seq", "proj"), ("groups", "chan")),
        P(("groups", "chan")),
    )
    return jax.shard_map(
        shards,
        mesh=mesh,
        in_specs=placed,
        out_specs=P(("seq", "proj"), ("groups", "chan")),
        check_vma=False,
    )
```

profile of v0, /device:TPU:0, one launch (start us, length us, event | category | flops | bytes accessed | tf_op | source)
XLA Modules:
  0.0 312.7 jit_solution(15190194606105853624)
XLA Ops:
  6.5 0.0 copy-start
  6.5 0.0 all-gather.2.cloned.1.call-start
  6.5 0.7 all-gather.2.cloned.1.call-update
  7.3 0.0 reduce-scatter.2.cloned.1.call-start
  7.3 1.1 copy-done
  8.4 2.9 copy.14
  11.3 30.4 %all-gather.2.cloned.1.call-done = bf16[2048,4096]{1,0:T(8,128)(2,1)} async-done(((bf16[2048,2048]{1,0:T(8,128)(2,1)}), bf16[2048,4096]{1,0:T(8,128)(2,1)}) %all-gather.2.cloned.1.call-update) | async-done | bytes 16777232 | tf_op jit(solution)/shard_map/all_gather | solution.py:62
  41.7 0.0 copy-start.1
  41.7 14.5 %fusion.186 = f32[2048,384]{1,0:T(8,128)} fusion(bf16[2048,4096]{1,0:T(8,128)(2,1)} %all-gather.2.cloned.1.call-done, bf16[4096,384]{0,1:T(8,128)(2,1)} %bitcast.120), kind=kOutput, calls=%fused_computation.202 | convolution fusion | flops 6442450944 | bytes 23068672 | tf_op jit(solution)/shard_map/dot_general | solution.py:68
  56.2 0.0 copy-start.2
  56.2 0.0 reduce-scatter.2.cloned.1.call-update
  56.2 0.0 copy-done.1
  56.2 0.9 copy.17
  57.1 5.8 %all-to-all-start.1 = ((bf16[8,16,1024]{2,1,0:T(8,128)(2,1)}), bf16[8,16,1024]{2,1,0:T(8,128)(2,1)S(1)}, u32[]{:S(2)}, u32[]{:S(2)}) async-start(bf16[8,16,1024]{2,1,0:T(8,128)(2,1)} %bitcast.8), calls=%async_computation.2 | async-start | bytes 524288 | tf_op jit(solution)/shard_map/all_to_all | solution.py:95
  62.9 0.1 broadcast_multiply_fusion
  63.0 0.1 fusion.80
  63.1 0.0 copy-done.2
  63.2 40.5 %reduce-scatter.2.cloned.1.call-done = f32[1024,384]{1,0:T(8,128)} async-done(((f32[2048,384]{1,0:T(8,128)}), f32[1024,384]{1,0:T(8,128)}) %reduce-scatter.2.cloned.1.call-update) | async-done | bytes 1572880 | tf_op jit(solution)/shard_map/reduce_scatter | solution.py:67
  103.7 0.7 slice.79
  104.4 2.2 collective-permute-start
  106.6 0.1 negate_sine_fusion
  106.8 1.1 collective-permute-done
  107.9 3.2 %fusion.45 = f32[1024,384]{1,0:T(8,128)S(1)} fusion(f32[2,384]{1,0:T(2,128)S(1)} %collective-permute-done, f32[1024,384]{1,0:T(8,128)} %reduce-scatter.2.cloned.1.call-done, f32[384]{0:T(512)S(1)} %get-tuple-element.16, f32[384]{0:T(512)S(1)} %get-tuple-element.17, f32[384]{0:T(512)S(1)} %get-tuple-element.15), kind=kLoop, calls=%fused_computation.48 | loop fusion | flops 2752512 | bytes 3153408 | tf_op jit(solution)/shard_map/add | solution.py:81
  111.2 0.1 fusion.193
  111.2 0.8 copy.15
  112.1 0.0 all-to-all-done.1
  112.1 8.0 %all-to-all-start = ((bf16[8,16,1024]{2,1,0:T(8,128)(2,1)}), bf16[8,16,1024]{2,1,0:T(8,128)(2,1)S(1)}, u32[]{:S(2)}, u32[]{:S(2)}) async-start(bf16[8,16,1024]{2,1,0:T(8,128)(2,1)} %bitcast.5), calls=%async_computation.1 | async-start | bytes 524288 | tf_op jit(solution)/shard_map/all_to_all | solution.py:94
  120.0 0.1 fusion.83
  120.2 0.1 fusion.76
  120.3 0.2 convert_bitcast_fusion
  120.5 7.3 %all-to-all-done = bf16[8,16,1024]{2,1,0:T(8,128)(2,1)S(1)} async-done(((bf16[8,16,1024]{2,1,0:T(8,128)(2,1)}), bf16[8,16,1024]{2,1,0:T(8,128)(2,1)S(1)}, u32[]{:S(2)}, u32[]{:S(2)}) %all-to-all-start) | async-done | bytes 262176 | tf_op jit(solution)/shard_map/all_to_all | solution.py:94
  127.8 0.2 convert_bitcast_fusion.1
  127.9 0.4 multiply_add_fusion.2
  128.3 1.2 fusion.63
  129.5 1.2 fusion.64
  130.8 1.3 fusion.41
  132.2 1.3 fusion.40
  133.5 19.1 %fusion.7 = f32[64,8,1024]{2,1,0:T(8,128)S(1)} fusion(f32[64,1024,8]{1,2,0:T(8,128)S(1)} %fusion.41, f32[64,1024,8]{1,2,0:T(8,128)S(1)} %fusion.40, f32[8,1024]{1,0:T(8,128)S(1)} %get-tuple-element.22, f32[8,1024]{1,0:T(8,128)S(1)} %get-tuple-element.23), kind=kOutput, calls=%fused_computation.10 | convolution fusion | flops 3238526976 | bytes 6356992 | tf_op jit(solution)/shard_map/ckj,jq->ckq/dot_general | solution.py:31
  152.6 19.1 %fusion.9 = f32[64,8,1024]{2,1,0:T(8,128)S(1)} fusion(f32[64,1024,8]{1,2,0:T(8,128)S(1)} %fusion.41, f32[64,1024,8]{1,2,0:T(8,128)S(1)} %fusion.40, f32[8,1024]{1,0:T(8,128)S(1)} %get-tuple-element.22, f32[8,1024]{1,0:T(8,128)S(1)} %get-tuple-element.23), kind=kOutput, calls=%fused_computation.12 | convolution fusion | flops 3238526976 | bytes 6356992 | tf_op jit(solution)/shard_map/ckj,jq->ckq/dot_general | solution.py:28
  171.7 18.8 %fusion.50 = f32[64,8,1024]{2,1,0:T(8,128)S(1)} fusion(f32[64,8,1024]{2,1,0:T(8,128)S(1)} %fusion.7, f32[64,1024,8]{1,2,0:T(8,128)S(1)} %fusion.41, f32[64,1024,8]{1,2,0:T(8,128)S(1)} %fusion.40, f32[8,1024]{1,0:T(8,128)S(1)} %get-tuple-element.22, f32[8,1024]{1,0:T(8,128)S(1)} %get-tuple-element.23), kind=kOutput, calls=%fused_computation.52 | convolution fusion | flops 3238002688 | bytes 8454144 | tf_op jit(solution)/shard_map/ckj,jq->ckq/dot_general | solution.py:31
  190.6 18.8 %fusion.47 = f32[64,8,1024]{2,1,0:T(8,128)S(1)} fusion(f32[64,8,1024]{2,1,0:T(8,128)S(1)} %fusion.9, f32[64,1024,8]{1,2,0:T(8,128)S(1)} %fusion.41, f32[64,1024,8]{1,2,0:T(8,128)S(1)} %fusion.40, f32[8,1024]{1,0:T(8,128)S(1)} %get-tuple-element.22, f32[8,1024]{1,0:T(8,128)S(1)} %get-tuple-element.23), kind=kOutput, calls=%fused_computation.51 | convolution fusion | flops 3238002688 | bytes 8454144 | tf_op jit(solution)/shard_map/ckj,jq->ckq/dot_general | solution.py:28
  209.4 0.5 multiply_add_fusion.1
  209.9 18.4 %fusion.3 = f32[32,8,1024]{2,1,0:T(8,128)S(1)} fusion(f32[32,8,1024]{2,1,0:T(8,128)S(1)} %get-tuple-element.6), kind=kOutput, calls=%fused_computation.6 | convolution fusion | flops 1625292800 | bytes 2097152 | tf_op jit(solution)/shard_map/ckq,qj->ckj/dot_general | solution.py:31
  228.3 18.2 %fusion.5 = f32[32,8,1024]{2,1,0:T(8,128)S(1)} fusion(f32[32,8,1024]{2,1,0:T(8,128)S(1)} %get-tuple-element.5), kind=kOutput, calls=%fused_computation.8 | convolution fusion | flops 1625292800 | bytes 2097152 | tf_op jit(solution)/shard_map/ckq,qj->ckj/dot_general | solution.py:28
  246.6 18.3 %fusion.60 = f32[32,8,1024]{2,1,0:T(8,128)S(1)} fusion(f32[32,8,1024]{2,1,0:T(8,128)S(1)} %fusion.3, f32[32,8,1024]{2,1,0:T(8,128)S(1)} %get-tuple-element.5), kind=kOutput, calls=%fused_computation.60 | convolution fusion | flops 1625554944 | bytes 3145728 | tf_op jit(solution)/shard_map/ckq,qj->ckj/dot_general | solution.py:31
  264.9 18.4 %fusion.57 = f32[32,8,1024]{2,1,0:T(8,128)S(1)} fusion(f32[32,8,1024]{2,1,0:T(8,128)S(1)} %fusion.5, f32[32,8,1024]{2,1,0:T(8,128)S(1)} %get-tuple-element.6), kind=kOutput, calls=%fused_computation.59 | convolution fusion | flops 1625554944 | bytes 3145728 | tf_op jit(solution)/shard_map/ckq,qj->ckj/dot_general | solution.py:28
  283.3 0.7 fusion.72
  284.0 0.7 fusion.71
  284.8 0.8 fusion.54
  285.7 0.3 copy.24
  286.0 0.8 fusion.56
  286.8 0.1 fusion.185
  286.9 0.0 copy-start.3
  286.9 0.3 copy.22
  287.2 0.3 copy.23
  287.5 0.1 subtract_multiply_fusion
  287.7 16.9 %all_to_all.45 = f32[16,8,1024]{2,0,1:T(8,128)S(1)} all-to-all(f32[16,8,1024]{2,0,1:T(8,128)S(1)} %bitcast.122), channel_id=1, replica_groups=mesh['groups'=2,'seq'=4,'proj'=2,'chan'=2] {'seq','proj'}, dimensions={1} | all-to-all | bytes 1048576 | tf_op jit(solution)/shard_map/all_to_all | solution.py:124
  304.6 0.2 copy.20
  304.8 0.0 copy-done.3
  304.8 0.8 fusion.70
  (4 shorter events, 0.1 us)
Async XLA Ops:
  6.5 1.9 copy-start
  6.5 35.2 %all-gather.2.cloned.1.call-start = ((), (), s32[]{:S(2)}) async-start(), calls=%async_computation.4 | async-start | bytes 25165824 | tf_op jit(solution)/shard_map/all_gather | solution.py:62
  7.3 96.5 %reduce-scatter.2.cloned.1.call-start = ((), (), s32[]{:S(2)}) async-start(), calls=%async_computation.5 | async-start | bytes 4718592 | tf_op jit(solution)/shard_map/reduce_scatter | solution.py:67
  41.7 14.5 %copy-start.1 = (bf16[1024,128]{1,0:T(8,128)(2,1)S(1)}, bf16[1024,128]{1,0:T(8,128)(2,1)}, u32[]{:S(2)}) copy-start(bf16[1024,128]{1,0:T(8,128)(2,1)} %param.8) | copy-start | bytes 786436
  56.2 6.9 %copy-start.2 = (f32[3,3,128]{2,1,0:T(4,128)S(1)}, f32[3,3,128]{2,1,0:T(4,128)}, u32[]{:S(2)}) copy-start(f32[3,3,128]{2,1,0:T(4,128)} %param.7) | copy-start | bytes 13828
  57.1 55.0 %all-to-all-start.1 = ((bf16[8,16,1024]{2,1,0:T(8,128)(2,1)}), bf16[8,16,1024]{2,1,0:T(8,128)(2,1)S(1)}, u32[]{:S(2)}, u32[]{:S(2)}) async-start(bf16[8,16,1024]{2,1,0:T(8,128)(2,1)} %bitcast.8), calls=%async_computation.2 | async-start | bytes 524288 | tf_op jit(solution)/shard_map/all_to_all | solution.py:95
  104.4 3.5 %collective-permute-start = (f32[2,384]{1,0:T(2,128)S(1)}, f32[2,384]{1,0:T(2,128)S(1)}, u32[]{:S(2)}, u32[]{:S(2)}) collective-permute-start(f32[2,384]{1,0:T(2,128)S(1)} %slice.79), channel_id=1, source_target_pairs={{0,2},{2,4},{4,6},{6,8},{8,10},{10,12},{12,14},{1,3},{3,5},{5,7},{... | collective-permute-start | bytes 9224 | tf_op jit(solution)/shard_map/ppermute | solution.py:13
  112.1 15.7 %all-to-all-start = ((bf16[8,16,1024]{2,1,0:T(8,128)(2,1)}), bf16[8,16,1024]{2,1,0:T(8,128)(2,1)S(1)}, u32[]{:S(2)}, u32[]{:S(2)}) async-start(bf16[8,16,1024]{2,1,0:T(8,128)(2,1)} %bitcast.5), calls=%async_computation.1 | async-start | bytes 524288 | tf_op jit(solution)/shard_map/all_to_all | solution.py:94
  286.9 17.9 %copy-start.3 = (f32[128]{0:T(128)S(1)}, f32[128]{0:T(128)}, u32[]{:S(2)}) copy-start(f32[128]{0:T(128)} %param.9) | copy-start | bytes 1540
Sparse Core Ops, SparseCore 0:
  8.9 32.7 all-gather.1
  56.4 47.3 reduce-scatter.1
where the time goes:
time: 317 us; the launch traced here: 313 us
  matrix products  172 us (54%)
  waiting for transfers between devices  80.1 us (25%)
  blocking collectives  16.9 us (5%)
  starting transfers between devices  16 us (5%)
  between operations  14 us (4%)
  local copies, waits for them, and re-layouts  7.73 us (2%)
  other arithmetic  6.06 us (2%)
    reduce_scatter x1, waiting for transfers between devices, shards(): lax.psum_scatter(jnp.dot(whole_cols, weights, preferred_element_type=jnp....  40.5 us
    dot_general x4, matrix products, complex_einsum(): jnp.einsum(form, left_re, right_im, precision=precise)  39.6 us
    dot_general x4, matrix products, complex_einsum(): jnp.einsum(form, left_im, right_im, precision=precise)  39.5 us
    dot_general x4, matrix products, complex_einsum(): jnp.einsum(form, left_re, right_re, precision=precise)  39.2 us
    dot_general x4, matrix products, complex_einsum(): jnp.einsum(form, left_im, right_re, precision=precise)  39.2 us
    all_gather x1, waiting for transfers between devices, shards(): whole_cols = lax.all_gather(tokens, 'chan', axis=1, tiled=True)  30.4 us
    all_to_all x1, blocking collectives, shards(): lax.all_to_all(long_cols, ('seq', 'proj'), split_axis=1, concat_axis=0, t...  16.9 us
    dot_general x1, matrix products, shards(): jnp.dot(whole_cols, weights, preferred_element_type=jnp.float32)  14.5 us
  transfers between devices with their start and end apart: 5, of which 4 were waited for; matrix products, arithmetic and copies ran while one was open for 3% of the time, Pallas kernels for 0%

commit v1 on v0

--- a/solution.py
+++ b/solution.py
@@ -121,7 +121,19 @@
     time_re = back_re.reshape(2 * per_device, seq_len) * (1.0 / seq_len)
     time_im = back_im.reshape(2 * per_device, seq_len) * (1.0 / seq_len)
     long_cols = combine_halves(time_re, time_im, per_device, full_angle, 0)
-    long_rows = lax.all_to_all(long_cols, ("seq", "proj"), split_axis=1, concat_axis=0, tiled=True)
+    ways, here = (lax.axis_size(("seq", "proj")), lax.axis_index(("seq", "proj")))
+    width_2 = long_cols.shape[1] // ways
+    shape = list(long_cols.shape)
+    shape[1] = width_2
+    height = shape[0]
+    shape[0] = height * ways
+    full = jnp.zeros(shape, long_cols.dtype)
+    for mask in range(ways):
+        part = lax.dynamic_slice_in_dim(long_cols, (here ^ mask) * width_2, width_2, axis=1)
+        if mask:
+            part = lax.ppermute(part, ("seq", "proj"), [(d, d ^ mask) for d in range(ways)])
+        full = lax.dynamic_update_slice_in_dim(full, part, (here ^ mask) * height, axis=0)
+    long_rows = full
     long_conv = long_rows.T
     result = query_part * (long_conv + filter_bias * gated_rows)
     return result.astype(jnp.bfloat16)

time: 317 us -> 415 us (1.31)
  the two profiles are of different devices: /device:TPU:0 before, /device:TPU:16 now
where the time goes in v1:
time: 415 us; the launch traced here: 410 us
  matrix products  172 us (41%)
  waiting for transfers between devices  137 us (33%)
  local copies, waits for them, and re-layouts  52.2 us (13%)
  starting transfers between devices  21.8 us (5%)
  between operations  14 us (3%)
  other arithmetic  13.4 us (3%)
    ppermute x7, waiting for transfers between devices, shards(): lax.ppermute(part, ('seq', 'proj'), [(d, d ^ mask) for d in range(ways)])  57.5 us
    reduce_scatter x1, waiting for transfers between devices, shards(): lax.psum_scatter(jnp.dot(whole_cols, weights, preferred_element_type=jnp....  40 us
    dot_general x4, matrix products, complex_einsum(): jnp.einsum(form, left_re, right_im, precision=precise)  39.9 us
    dot_general x4, matrix products, complex_einsum(): jnp.einsum(form, left_im, right_re, precision=precise)  39.6 us
    dot_general x4, matrix products, complex_einsum(): jnp.einsum(form, left_im, right_im, precision=precise)  39.2 us
    dot_general x4, matrix products, complex_einsum(): jnp.einsum(form, left_re, right_re, precision=precise)  38.7 us
    dynamic_update_slice x8, local copies, waits for them, and re-layouts, shards(): lax.dynamic_update_slice_in_dim(full, part, (here ^ mask) * height, axis=0)  32.3 us
    all_gather x1, waiting for transfers between devices, shards(): whole_cols = lax.all_gather(tokens, 'chan', axis=1, tiled=True)  29.1 us
  transfers between devices with their start and end apart: 12, of which 9 were waited for; matrix products, arithmetic and copies ran while one was open for 9% of the time, Pallas kernels for 0%

profile of v1, /device:TPU:16, one launch (start us, length us, event | category | flops | bytes accessed | tf_op | source)
XLA Modules:
  0.0 410.0 jit_solution(14977432995523463204)
XLA Ops:
  6.5 0.7 all-gather.2.cloned.1.call-update
  7.3 1.1 copy-done.2
  8.4 2.8 copy.18
  11.3 29.1 %all-gather.2.cloned.1.call-done = bf16[2048,4096]{1,0:T(8,128)(2,1)} async-done(((bf16[2048,2048]{1,0:T(8,128)(2,1)}), bf16[2048,4096]{1,0:T(8,128)(2,1)}) %all-gather.2.cloned.1.call-update) | async-done | bytes 16777232 | tf_op jit(solution)/shard_map/all_gather | solution.py:62
  40.4 14.5 %fusion.189 = f32[2048,384]{1,0:T(8,128)} fusion(bf16[2048,4096]{1,0:T(8,128)(2,1)} %all-gather.2.cloned.1.call-done, bf16[4096,384]{0,1:T(8,128)(2,1)} %bitcast.121), kind=kOutput, calls=%fused_computation.213 | convolution fusion | flops 6442450944 | bytes 23068672 | tf_op jit(solution)/shard_map/dot_general | solution.py:68
  54.9 0.9 copy.21
  55.7 6.0 %all-to-all-start.1 = ((bf16[8,16,1024]{2,1,0:T(8,128)(2,1)}), bf16[8,16,1024]{2,1,0:T(8,128)(2,1)S(1)}, u32[]{:S(2)}, u32[]{:S(2)}) async-start(bf16[8,16,1024]{2,1,0:T(8,128)(2,1)} %bitcast.8), calls=%async_computation.2 | async-start | bytes 524288 | tf_op jit(solution)/shard_map/all_to_all | solution.py:95
  62.1 40.0 %reduce-scatter.2.cloned.1.call-done = f32[1024,384]{1,0:T(8,128)} async-done(((f32[2048,384]{1,0:T(8,128)}), f32[1024,384]{1,0:T(8,128)}) %reduce-scatter.2.cloned.1.call-update) | async-done | bytes 1572880 | tf_op jit(solution)/shard_map/reduce_scatter | solution.py:67
  102.1 0.7 slice.79
  102.8 2.4 collective-permute-start
  105.3 0.1 negate_sine_fusion
  105.5 3.7 collective-permute-done
  109.2 3.0 fusion.48
  112.2 1.1 copy-done
  113.4 0.8 copy.19
  114.2 5.3 %all-to-all-start = ((bf16[8,16,1024]{2,1,0:T(8,128)(2,1)}), bf16[8,16,1024]{2,1,0:T(8,128)(2,1)S(1)}, u32[]{:S(2)}, u32[]{:S(2)}) async-start(bf16[8,16,1024]{2,1,0:T(8,128)(2,1)} %bitcast.5), calls=%async_computation.1 | async-start | bytes 524288 | tf_op jit(solution)/shard_map/all_to_all | solution.py:94
  119.8 0.2 convert_bitcast_fusion
  120.0 5.5 %all-to-all-done = bf16[8,16,1024]{2,1,0:T(8,128)(2,1)S(1)} async-done(((bf16[8,16,1024]{2,1,0:T(8,128)(2,1)}), bf16[8,16,1024]{2,1,0:T(8,128)(2,1)S(1)}, u32[]{:S(2)}, u32[]{:S(2)}) %all-to-all-start) | async-done | bytes 262176 | tf_op jit(solution)/shard_map/all_to_all | solution.py:94
  125.5 0.2 convert_bitcast_fusion.1
  125.6 0.3 multiply_add_fusion.2
  126.0 1.2 fusion.66
  127.2 1.2 fusion.67
  128.5 1.3 fusion.44
  129.9 1.3 fusion.43
  131.2 19.3 %fusion.10 = f32[64,8,1024]{2,1,0:T(8,128)S(1)} fusion(f32[64,1024,8]{1,2,0:T(8,128)S(1)} %fusion.44, f32[64,1024,8]{1,2,0:T(8,128)S(1)} %fusion.43, f32[8,1024]{1,0:T(8,128)S(1)} %get-tuple-element.30, f32[8,1024]{1,0:T(8,128)S(1)} %get-tuple-element.31), kind=kOutput, calls=%fused_computation.15 | convolution fusion | flops 3238526976 | bytes 6356992 | tf_op jit(solution)/shard_map/ckj,jq->ckq/dot_general | solution.py:31
  150.6 18.9 %fusion.12 = f32[64,8,1024]{2,1,0:T(8,128)S(1)} fusion(f32[64,1024,8]{1,2,0:T(8,128)S(1)} %fusion.44, f32[64,1024,8]{1,2,0:T(8,128)S(1)} %fusion.43, f32[8,1024]{1,0:T(8,128)S(1)} %get-tuple-element.30, f32[8,1024]{1,0:T(8,128)S(1)} %get-tuple-element.31), kind=kOutput, calls=%fused_computation.17 | convolution fusion | flops 3238526976 | bytes 6356992 | tf_op jit(solution)/shard_map/ckj,jq->ckq/dot_general | solution.py:28
  169.5 19.0 %fusion.53 = f32[64,8,1024]{2,1,0:T(8,128)S(1)} fusion(f32[64,8,1024]{2,1,0:T(8,128)S(1)} %fusion.10, f32[64,1024,8]{1,2,0:T(8,128)S(1)} %fusion.44, f32[64,1024,8]{1,2,0:T(8,128)S(1)} %fusion.43, f32[8,1024]{1,0:T(8,128)S(1)} %get-tuple-element.30, f32[8,1024]{1,0:T(8,128)S(1)} %get-tuple-element.31), kind=kOutput, calls=%fused_computation.57 | convolution fusion | flops 3238002688 | bytes 8454144 | tf_op jit(solution)/shard_map/ckj,jq->ckq/dot_general | solution.py:31
  188.5 18.6 %fusion.50 = f32[64,8,1024]{2,1,0:T(8,128)S(1)} fusion(f32[64,8,1024]{2,1,0:T(8,128)S(1)} %fusion.12, f32[64,1024,8]{1,2,0:T(8,128)S(1)} %fusion.44, f32[64,1024,8]{1,2,0:T(8,128)S(1)} %fusion.43, f32[8,1024]{1,0:T(8,128)S(1)} %get-tuple-element.30, f32[8,1024]{1,0:T(8,128)S(1)} %get-tuple-element.31), kind=kOutput, calls=%fused_computation.56 | convolution fusion | flops 3238002688 | bytes 8454144 | tf_op jit(solution)/shard_map/ckj,jq->ckq/dot_general | solution.py:28
  207.1 0.5 multiply_add_fusion.1
  207.6 18.4 %fusion.6 = f32[32,8,1024]{2,1,0:T(8,128)S(1)} fusion(f32[32,8,1024]{2,1,0:T(8,128)S(1)} %get-tuple-element.14), kind=kOutput, calls=%fused_computation.11 | convolution fusion | flops 1625292800 | bytes 2097152 | tf_op jit(solution)/shard_map/ckq,qj->ckj/dot_general | solution.py:31
  226.1 18.2 %fusion.8 = f32[32,8,1024]{2,1,0:T(8,128)S(1)} fusion(f32[32,8,1024]{2,1,0:T(8,128)S(1)} %get-tuple-element.13), kind=kOutput, calls=%fused_computation.13 | convolution fusion | flops 1625292800 | bytes 2097152 | tf_op jit(solution)/shard_map/ckq,qj->ckj/dot_general | solution.py:28
  244.3 18.5 %fusion.63 = f32[32,8,1024]{2,1,0:T(8,128)S(1)} fusion(f32[32,8,1024]{2,1,0:T(8,128)S(1)} %fusion.6, f32[32,8,1024]{2,1,0:T(8,128)S(1)} %get-tuple-element.13), kind=kOutput, calls=%fused_computation.65 | convolution fusion | flops 1625554944 | bytes 3145728 | tf_op jit(solution)/shard_map/ckq,qj->ckj/dot_general | solution.py:31
  262.9 18.1 %fusion.60 = f32[32,8,1024]{2,1,0:T(8,128)S(1)} fusion(f32[32,8,1024]{2,1,0:T(8,128)S(1)} %fusion.8, f32[32,8,1024]{2,1,0:T(8,128)S(1)} %get-tuple-element.14), kind=kOutput, calls=%fused_computation.64 | convolution fusion | flops 1625554944 | bytes 3145728 | tf_op jit(solution)/shard_map/ckq,qj->ckj/dot_general | solution.py:28
  281.0 0.7 fusion.75
  281.8 0.7 fusion.74
  282.5 0.8 fusion.57
  283.3 0.8 slice.91
  284.2 3.7 copy.25
  287.9 0.8 fusion.59
  288.8 2.7 copy.24
  291.5 2.6 copy.23
  294.1 7.7 %fusion.4 = f32[16,8192]{0,1:T(8,128)S(1)} fusion(f32[16,8,1024]{0,2,1:T(8,128)} %copy.25, f32[16,8,1024]{0,2,1:T(8,128)} %copy.24, f32[16,8,1024]{0,2,1:T(8,128)} %copy.23, f32[8192]{0:T(1024)S(1)} %get-tuple-element.34, f32[8192]{0:T(1024)S(1)} %get-tuple-element.35), kind=kLoop, calls=%fused_computation.8 | loop fusion | flops 655360 | bytes 2162688 | tf_op jit(solution)/shard_map/mul | solution.py:58
  301.8 1.6 constant_dynamic-slice_fusion
  303.4 0.2 collective-permute-start.1
  303.6 2.1 collective-permute-start.2
  305.8 1.1 collective-permute-start.3
  306.9 2.1 collective-permute-start.4
  309.0 0.8 collective-permute-start.5
  309.8 7.2 %collective-permute-done.1 = f32[16,1024]{0,1:T(8,128)S(1)} collective-permute-done((f32[16,1024]{0,1:T(8,128)S(1)}, f32[16,1024]{0,1:T(8,128)S(1)}, u32[]{:S(2)}, u32[]{:S(2)}) %collective-permute-start.1) | collective-permute-done | bytes 65568 | tf_op jit(solution)/shard_map/ppermute | solution.py:134
  317.0 1.4 collective-permute-start.6
  318.4 19.2 %collective-permute-done.2 = f32[16,1024]{0,1:T(8,128)S(1)} collective-permute-done((f32[16,1024]{0,1:T(8,128)S(1)}, f32[16,1024]{0,1:T(8,128)S(1)}, u32[]{:S(2)}, u32[]{:S(2)}) %collective-permute-start.2) | collective-permute-done | bytes 65568 | tf_op jit(solution)/shard_map/ppermute | solution.py:134
  337.6 0.8 copy-done.4
  338.6 3.1 dynamic_update_slice.24
  341.7 4.5 %dynamic_update_slice.25 = f32[128,1024]{0,1:T(8,128)S(1)} dynamic-update-slice(f32[128,1024]{0,1:T(8,128)S(1)} %dynamic_update_slice.24, f32[16,1024]{0,1:T(8,128)} %copy-done.3, s32[]{:T(128)S(6)} %select_n.132, s32[]{:T(128)} %constant.75.clone.1) | dynamic-update-slice | bytes 131076 | tf_op jit(solution)/shard_map/dynamic_update_slice | solution.py:135
  346.2 4.5 %dynamic_update_slice.26 = f32[128,1024]{0,1:T(8,128)S(1)} dynamic-update-slice(f32[128,1024]{0,1:T(8,128)S(1)} %dynamic_update_slice.25, f32[16,1024]{0,1:T(8,128)} %copy-done.4, s32[]{:T(128)S(6)} %select_n.134, s32[]{:T(128)} %constant.75.clone.1) | dynamic-update-slice | bytes 131076 | tf_op jit(solution)/shard_map/dynamic_update_slice | solution.py:135
  350.7 4.5 %dynamic_update_slice.27 = f32[128,1024]{0,1:T(8,128)S(1)} dynamic-update-slice(f32[128,1024]{0,1:T(8,128)S(1)} %dynamic_update_slice.26, f32[16,1024]{0,1:T(8,128)} %collective-permute-done.3, s32[]{:T(128)S(6)} %select_n.136, s32[]{:T(128)} %constant.75.clone.1) | dynamic-update-slice | bytes 131076 | tf_op jit(solution)/shard_map/dynamic_update_slice | solution.py:135
  355.2 3.9 dynamic_update_slice.28
  359.1 18.7 %collective-permute-done.5 = f32[16,1024]{0,1:T(8,128)} collective-permute-done((f32[16,1024]{0,1:T(8,128)}, f32[16,1024]{0,1:T(8,128)}, u32[]{:S(2)}, u32[]{:S(2)}) %collective-permute-start.5) | collective-permute-done | bytes 65568 | tf_op jit(solution)/shard_map/ppermute | solution.py:134
  377.9 4.4 %dynamic_update_slice.29 = f32[128,1024]{0,1:T(8,128)S(1)} dynamic-update-slice(f32[128,1024]{0,1:T(8,128)S(1)} %dynamic_update_slice.28, f32[16,1024]{0,1:T(8,128)} %collective-permute-done.5, s32[]{:T(128)S(6)} %select_n.140, s32[]{:T(128)} %constant.75.clone.1) | dynamic-update-slice | bytes 131076 | tf_op jit(solution)/shard_map/dynamic_update_slice | solution.py:135
  382.3 7.3 %collective-permute-done.6 = f32[16,1024]{0,1:T(8,128)} collective-permute-done((f32[16,1024]{0,1:T(8,128)}, f32[16,1024]{0,1:T(8,128)}, u32[]{:S(2)}, u32[]{:S(2)}) %collective-permute-start.6) | collective-permute-done | bytes 65568 | tf_op jit(solution)/shard_map/ppermute | solution.py:134
  389.6 4.4 %dynamic_update_slice.30 = f32[128,1024]{0,1:T(8,128)S(1)} dynamic-update-slice(f32[128,1024]{0,1:T(8,128)S(1)} %dynamic_update_slice.29, f32[16,1024]{0,1:T(8,128)} %collective-permute-done.6, s32[]{:T(128)S(6)} %select_n.142, s32[]{:T(128)} %constant.75.clone.1) | dynamic-update-slice | bytes 131076 | tf_op jit(solution)/shard_map/dynamic_update_slice | solution.py:135
  394.1 5.1 %collective-permute-done.7 = f32[16,1024]{0,1:T(8,128)S(1)} collective-permute-done((f32[16,1024]{0,1:T(8,128)}, f32[16,1024]{0,1:T(8,128)S(1)}, u32[]{:S(2)}, u32[]{:S(2)}) %collective-permute-start.7) | collective-permute-done | bytes 65568 | tf_op jit(solution)/shard_map/ppermute | solution.py:134
  399.1 3.0 dynamic_update_slice.31
  402.1 0.8 fusion.73
  (29 shorter events, 1.0 us)
Async XLA Ops:
  6.5 1.9 copy-start.2
  6.5 33.8 %all-gather.2.cloned.1.call-start = ((), (), s32[]{:S(2)}) async-start(), calls=%async_computation.3 | async-start | bytes 25165824 | tf_op jit(solution)/shard_map/all_gather | solution.py:62
  7.3 94.8 %reduce-scatter.2.cloned.1.call-start = ((), (), s32[]{:S(2)}) async-start(), calls=%async_computation.4 | async-start | bytes 4718592 | tf_op jit(solution)/shard_map/reduce_scatter | solution.py:67
  40.4 14.5 %copy-start.5 = (bf16[1024,128]{1,0:T(8,128)(2,1)S(1)}, bf16[1024,128]{1,0:T(8,128)(2,1)}, u32[]{:S(2)}) copy-start(bf16[1024,128]{1,0:T(8,128)(2,1)} %param.8) | copy-start | bytes 786436
  54.8 7.2 %copy-start.6 = (f32[3,3,128]{2,1,0:T(4,128)S(1)}, f32[3,3,128]{2,1,0:T(4,128)}, u32[]{:S(2)}) copy-start(f32[3,3,128]{2,1,0:T(4,128)} %param.7) | copy-start | bytes 13828
  55.7 58.5 %all-to-all-start.1 = ((bf16[8,16,1024]{2,1,0:T(8,128)(2,1)}), bf16[8,16,1024]{2,1,0:T(8,128)(2,1)S(1)}, u32[]{:S(2)}, u32[]{:S(2)}) async-start(bf16[8,16,1024]{2,1,0:T(8,128)(2,1)} %bitcast.8), calls=%async_computation.2 | async-start | bytes 524288 | tf_op jit(solution)/shard_map/all_to_all | solution.py:95
  102.8 6.4 %collective-permute-start = (f32[2,384]{1,0:T(2,128)S(1)}, f32[2,384]{1,0:T(2,128)S(1)}, u32[]{:S(2)}, u32[]{:S(2)}) collective-permute-start(f32[2,384]{1,0:T(2,128)S(1)} %slice.79), channel_id=1, source_target_pairs={{0,2},{2,4},{4,6},{6,8},{8,10},{10,12},{12,14},{1,3},{3,5},{5,7},{... | collective-permute-start | bytes 9224 | tf_op jit(solution)/shard_map/ppermute | solution.py:13
  112.2 1.1 copy-start
  114.2 11.2 %all-to-all-start = ((bf16[8,16,1024]{2,1,0:T(8,128)(2,1)}), bf16[8,16,1024]{2,1,0:T(8,128)(2,1)S(1)}, u32[]{:S(2)}, u32[]{:S(2)}) async-start(bf16[8,16,1024]{2,1,0:T(8,128)(2,1)} %bitcast.5), calls=%async_computation.1 | async-start | bytes 524288 | tf_op jit(solution)/shard_map/all_to_all | solution.py:94
  303.4 13.6 %collective-permute-start.1 = (f32[16,1024]{0,1:T(8,128)S(1)}, f32[16,1024]{0,1:T(8,128)S(1)}, u32[]{:S(2)}, u32[]{:S(2)}) collective-permute-start(f32[16,1024]{0,1:T(8,128)S(1)} %get-tuple-element.11), channel_id=1, source_target_pairs={{0,2},{2,0},{4,6},{6,4},{8,10},{10,8},{12,14},{14,12},{1,3},{3,1},... | collective-permute-start | bytes 196616 | tf_op jit(solution)/shard_map/ppermute | solution.py:134
  303.6 34.0 %collective-permute-start.2 = (f32[16,1024]{0,1:T(8,128)S(1)}, f32[16,1024]{0,1:T(8,128)S(1)}, u32[]{:S(2)}, u32[]{:S(2)}) collective-permute-start(f32[16,1024]{0,1:T(8,128)S(1)} %get-tuple-element.10), channel_id=1, source_target_pairs={{0,4},{2,6},{4,0},{6,2},{8,12},{10,14},{12,8},{14,10},{1,5},{3,7},... | collective-permute-start | bytes 196616 | tf_op jit(solution)/shard_map/ppermute | solution.py:134
  305.8 44.9 %collective-permute-start.3 = (f32[16,1024]{0,1:T(8,128)}, f32[16,1024]{0,1:T(8,128)}, u32[]{:S(2)}, u32[]{:S(2)}) collective-permute-start(f32[16,1024]{0,1:T(8,128)} %get-tuple-element.9), channel_id=1, source_target_pairs={{0,6},{2,4},{4,2},{6,0},{8,14},{10,12},{12,10},{14,8},{1,7},{3,5},... | collective-permute-start | bytes 196616 | tf_op jit(solution)/shard_map/ppermute | solution.py:134
  306.9 48.3 %collective-permute-start.4 = (f32[16,1024]{0,1:T(8,128)}, f32[16,1024]{0,1:T(8,128)}, u32[]{:S(2)}, u32[]{:S(2)}) collective-permute-start(f32[16,1024]{0,1:T(8,128)} %get-tuple-element.8), channel_id=1, source_target_pairs={{0,8},{2,10},{4,12},{6,14},{8,0},{10,2},{12,4},{14,6},{1,9},{3,11}... | collective-permute-start | bytes 196616 | tf_op jit(solution)/shard_map/ppermute | solution.py:134
  309.0 68.9 %collective-permute-start.5 = (f32[16,1024]{0,1:T(8,128)}, f32[16,1024]{0,1:T(8,128)}, u32[]{:S(2)}, u32[]{:S(2)}) collective-permute-start(f32[16,1024]{0,1:T(8,128)} %get-tuple-element.7), channel_id=1, source_target_pairs={{0,10},{2,8},{4,14},{6,12},{8,2},{10,0},{12,6},{14,4},{1,11},{3,9}... | collective-permute-start | bytes 196616 | tf_op jit(solution)/shard_map/ppermute | solution.py:134
  317.0 20.6 %copy-start.3 = (f32[16,1024]{0,1:T(8,128)}, f32[16,1024]{0,1:T(8,128)S(1)}, u32[]{:S(2)}) copy-start(f32[16,1024]{0,1:T(8,128)S(1)} %collective-permute-done.1) | copy-start | bytes 196612
  317.0 72.6 %collective-permute-start.6 = (f32[16,1024]{0,1:T(8,128)}, f32[16,1024]{0,1:T(8,128)}, u32[]{:S(2)}, u32[]{:S(2)}) collective-permute-start(f32[16,1024]{0,1:T(8,128)} %get-tuple-element.6), channel_id=1, source_target_pairs={{0,12},{2,14},{4,8},{6,10},{8,4},{10,6},{12,0},{14,2},{1,13},{3,15... | collective-permute-start | bytes 196616 | tf_op jit(solution)/shard_map/ppermute | solution.py:134
  337.6 0.8 copy-start.4
  338.4 60.7 %collective-permute-start.7 = (f32[16,1024]{0,1:T(8,128)}, f32[16,1024]{0,1:T(8,128)S(1)}, u32[]{:S(2)}, u32[]{:S(2)}) collective-permute-start(f32[16,1024]{0,1:T(8,128)} %get-tuple-element.5), channel_id=1, source_target_pairs={{0,14},{2,12},{4,10},{6,8},{8,6},{10,4},{12,2},{14,0},{1,15},{3,13... | collective-permute-start | bytes 196616 | tf_op jit(solution)/shard_map/ppermute | solution.py:134
  338.6 63.5 %copy-start.1 = (f32[1024,384]{1,0:T(8,128)S(1)}, f32[1024,384]{1,0:T(8,128)}, u32[]{:S(2)}) copy-start(f32[1024,384]{1,0:T(8,128)} %copy-done) | copy-start | bytes 4718596
  338.6 63.5 %copy-start.7 = (f32[128]{0:T(128)S(1)}, f32[128]{0:T(128)}, u32[]{:S(2)}) copy-start(f32[128]{0:T(128)} %param.9) | copy-start | bytes 1540
Sparse Core Ops, SparseCore 0:
  8.9 31.3 all-gather.1
  55.0 47.0 reduce-scatter.1
